TPU v7x, 32 devices: a whole 2x2x4 slice. The times are simulated.
32 devices in a mesh: stream: 16 (over z, y, x), cross: 2 (over core).
Axes of the slice: x: 2, y: 2, z: 4, core: 2. Of those that a mesh axis runs over, the one named last changes fastest.
Arguments:
- vector: float32 [64, 4, 320], P('stream', 'cross'), may hold values from -2.5 to 2.5
- inverses: float32 [64, 4, 320, 320], P('stream', 'cross'), may hold values from -0.04 to 1
- lift_maps: float32 [4, 320, 80], replicated, may hold values from -1 to 1
- jacobians: float32 [64, 4, 4, 5, 5, 16], P('stream', 'cross'), may hold values from -0.2 to 1.43
- orient: int32 [64, 4], P('stream', 'cross'), may hold values from 0 to 7
Outputs:
- solution: float32 [64, 4, 320], P('stream', 'cross')
All inputs are finite; a program needn't handle non-finite values.
Results may differ from a plain program's by a relative error of at most 0.0003.
Values sent between devices are 32-bit elements; how exact they have to be, the bound alone decides.
A program may use at most 64 MiB of HBM per device.

v0:
```python
import functools

import jax
import jax.numpy as jnp
import numpy as np
from jax import lax
from jax.experimental import pallas as pl
from jax.experimental.pallas import tpu as pltpu
from jax.sharding import PartitionSpec as P

ORDER = 3
EXTENT = ORDER + 1
VARS = 5
FACE = EXTENT * EXTENT
TRACE = VARS * FACE
BLOCK = VARS * FACE * EXTENT
SLOTS = (0, EXTENT - 1) + tuple(range(1, EXTENT - 1))
WIDE = 256
ROWS = TRACE + 8
F32 = jnp.float32
BF16 = jnp.bfloat16


def split(value):
    high = value.astype(BF16)
    return high, (value - high.astype(F32)).astype(BF16)


def product(left, right, transposed=False):
    dims = (((1,), (1 if transposed else 0,)), ((), ()))
    dot = functools.partial(lax.dot_general, dimension_numbers=dims, preferred_element_type=F32)
    left_high, left_low = left
    right_high, right_low = right
    return dot(left_high, right_high) + (dot(left_high, right_low) + dot(left_low, right_high))


def lanes(shape):
    return lax.broadcasted_iota(jnp.int32, shape, 1)


def rows(shape):
    return lax.broadcasted_iota(jnp.int32, shape, 0)


def keep(mask, value):
    return jnp.where(mask, value, 0.0)


def join(left, right):
    lane = lanes((TRACE, WIDE))
    through = jnp.concatenate(
        [jnp.zeros((TRACE, WIDE), F32), keep(lane < 2 * TRACE, right[:TRACE])], axis=0
    )
    first = product(split(left[:, : 2 * TRACE]), split(through))
    lane_all = lanes((ROWS, WIDE))
    row_all = rows((ROWS, WIDE))
    first = first + keep((lane_all >= 2 * TRACE) | (row_all >= TRACE), right)
    back = left[:TRACE]
    moved = pltpu.roll(back, WIDE - 2 * TRACE, 1)
    through = jnp.concatenate(
        [
            keep(lane < TRACE, moved),
            jnp.zeros((TRACE, WIDE), F32),
            keep(lane >= 2 * TRACE, back),
        ],
        axis=0,
    )
    second = product(split(first[:, : 3 * TRACE]), split(through))
    middle = (lane_all >= TRACE) & (lane_all < 2 * TRACE)
    return second + keep(middle, first) + keep(lane_all < TRACE, left)


def apply(column, matrix):
    return jnp.sum(column * matrix, axis=0, keepdims=True)


def stack(parts):
    total = jnp.zeros((8, parts[0].shape[1]), F32)
    row = rows(total.shape)
    for index, part in enumerate(parts):
        total = jnp.where(row == index, jnp.broadcast_to(part, total.shape), total)
    return total


def to_low(value):
    return keep(lanes(value.shape) < TRACE, pltpu.roll(value, WIDE - 2 * TRACE, 1))


def rise(z_left, z_right, left, right):
    lane = lanes((8, WIDE))
    column = z_left.T
    first = z_right + keep(
        lane < 2 * TRACE,
        stack([apply(column[TRACE : 2 * TRACE, c : c + 1], m) for c, m in enumerate(right)]),
    )
    column = first.T
    second = stack([apply(column[:TRACE, c : c + 1], m) for c, m in enumerate(left)])
    return to_low(second) + keep(lane < TRACE, z_left) + keep(lane >= TRACE, first)


def descend(z_in, z_left, z_right, left, right):
    lane = lanes((8, WIDE))
    high = (lane >= TRACE) & (lane < 2 * TRACE)
    column = z_in.T
    inner = keep(
        high,
        z_left + stack([apply(column[TRACE : 2 * TRACE, c : c + 1], m) for c, m in enumerate(left)]),
    )
    passed = stack([apply(column[:TRACE, c : c + 1], m) for c, m in enumerate(right)])
    column = inner.T
    turned = stack([apply(column[TRACE : 2 * TRACE, c : c + 1], m) for c, m in enumerate(right)])
    low = keep(lane < TRACE, z_right + turned) + to_low(passed)
    return low + keep(high, z_in), keep(lane < TRACE, z_in) + inner


def kernel(
    layers, cells, count, width, rounds,
    inv, lhs, faces, pick, out,
    blocks, block_sem, lhs_high, lhs_low, lifted, ends, sides, y, x,
    nodes, z_nodes, mine, theirs, send_sem, recv_sem, tail_sems,
    z_mine, z_theirs, z_send, z_recv,
    traces, backs, got_high, got_back, from_left, from_right, cross_sems,
):
    elements = layers * cells
    place = lax.axis_index("stream")
    column_at = lax.axis_index("cross")
    local = layers.bit_length() - 1

    copies = []
    for e in range(elements):
        for slot, i in enumerate(SLOTS):
            copy = pltpu.make_async_copy(inv.at[e, :, i], blocks.at[e, slot], block_sem.at[e, slot])
            copy.start()

    bits = [lax.rem(place // (1 << k), 2) for k in range(rounds)]
    partners = [place + (1 - 2 * bits[k]) * (1 << k) for k in range(rounds)]
    barrier = pltpu.get_barrier_semaphore()
    for k in range(rounds):
        pl.semaphore_signal(barrier, inc=1, device_id=(partners[k], column_at), device_id_type=pl.DeviceIdType.MESH)

    @pl.when(column_at > 0)
    def _():
        pl.semaphore_signal(barrier, inc=1, device_id=(place, column_at - 1), device_id_type=pl.DeviceIdType.MESH)

    @pl.when(column_at < width - 1)
    def _():
        pl.semaphore_signal(barrier, inc=1, device_id=(place, column_at + 1), device_id_type=pl.DeviceIdType.MESH)

    high, low = split(lhs[...])
    lhs_high[...] = high
    lhs_low[...] = low
    z_nodes[...] = jnp.zeros_like(z_nodes)
    z_mine[...] = jnp.zeros_like(z_mine)
    backs[...] = jnp.zeros_like(backs)

    lane = lanes((TRACE, WIDE))

    def prepare(e, carry):
        for slot, i in enumerate(SLOTS):
            pltpu.make_async_copy(inv.at[e, :, i], blocks.at[e, slot], block_sem.at[e, slot]).wait()
        block = split(blocks[e].reshape(BLOCK, BLOCK))
        through = product((lhs_high[...], lhs_low[...]), block, transposed=True)
        row_values = through[4 * TRACE : 4 * TRACE + elements]
        own = jnp.sum(keep(rows(row_values.shape) == e, row_values), axis=0, keepdims=True)
        y[pl.ds(e, 1), :] = own
        lifted[e] = through[2 * TRACE : 4 * TRACE]
        upward = -product(split(faces[e, 0]), split(through[:TRACE]))
        downward = -product(split(faces[e, 1]), split(through[TRACE : 2 * TRACE]))
        ends[e, :TRACE] = downward
        ends[e, TRACE:] = upward
        matrix = keep(lane < 2 * TRACE, upward[:, :WIDE]) + pltpu.roll(
            keep(lane < TRACE, downward[:, :WIDE]), 2 * TRACE, 1
        )
        nodes[e, :TRACE] = matrix
        bottom = keep(lanes((8, WIDE)) < 2 * TRACE, jnp.broadcast_to(own[:, :WIDE], (8, WIDE)))
        nodes[e, TRACE:] = keep(rows((8, WIDE)) == 0, bottom)
        return carry

    lax.fori_loop(0, elements, prepare, 0)

    starts = []
    base = 0
    for level in range(local + 1):
        starts.append(base)
        base += layers >> level

    def node(level, index, c):
        return (starts[level] + index) * cells + c

    for level in range(local):
        for index in range(layers >> (level + 1)):
            for c in range(cells):
                nodes[node(level + 1, index, c)] = join(
                    nodes[node(level, 2 * index, c)], nodes[node(level, 2 * index + 1, c)]
                )
    for c in range(cells):
        mine[0, c] = nodes[node(local, 0, c)]

    sides_met = jnp.minimum(column_at, 1) + jnp.minimum(width - 1 - column_at, 1)
    pl.semaphore_wait(barrier, rounds + sides_met)

    def remote(source, target, send, recv, device):
        return pltpu.make_async_remote_copy(
            src_ref=source, dst_ref=target, send_sem=send, recv_sem=recv,
            device_id=device, device_id_type=pl.DeviceIdType.MESH,
        )

    def prepare_sides(e, carry):
        for side in range(2):
            span = slice(side * TRACE, (side + 1) * TRACE)
            sides[e, span] = product(split(faces[e, 2 + side]), split(lifted[e, span]))
        return carry

    sent = []
    for k in range(rounds):
        device = (partners[k], column_at)
        if k < rounds - 1:
            pending = [remote(mine.at[k], theirs.at[k], send_sem.at[k], recv_sem.at[k], device)]
        else:
            pending = [
                remote(
                    mine.at[k, :, :, pl.ds(0, 128)], theirs.at[k, :, :, pl.ds(0, 128)],
                    send_sem.at[k], recv_sem.at[k], device,
                ),
                remote(
                    mine.at[k, :, pl.ds(TRACE, 8), pl.ds(128, 128)],
                    theirs.at[k, :, pl.ds(TRACE, 8), pl.ds(128, 128)],
                    tail_sems.at[0], tail_sems.at[1], device,
                ),
            ]
        for copy in pending:
            copy.start()
        sent += pending
        if k == 0:
            lax.fori_loop(0, elements, prepare_sides, 0)
        for copy in pending:
            copy.wait_recv()
        if k < rounds - 1:
            flag = bits[k] == 1
            for c in range(cells):
                ours, other = mine[k, c], theirs[k, c]
                mine[k + 1, c] = join(jnp.where(flag, other, ours), jnp.where(flag, ours, other))

    def ordered(k, c):
        flag = bits[k] == 1
        ours, other = mine[k, c, :TRACE], theirs[k, c, :TRACE]
        return jnp.where(flag, other, ours), jnp.where(flag, ours, other)

    def fall(z_pairs):
        lane_z = lanes((8, WIDE))
        z_in = None
        for k in reversed(range(rounds)):
            flag = bits[k] == 1
            ours, other = z_pairs[k]
            z_left, z_right = jnp.where(flag, other, ours), jnp.where(flag, ours, other)
            if z_in is None:
                column = z_left.T
                turned = stack([
                    apply(column[TRACE : 2 * TRACE, c : c + 1], theirs[k, c, :TRACE, :128])
                    for c in range(cells)
                ])
                turned = jnp.concatenate([turned, jnp.zeros((8, WIDE - 128), F32)], axis=1)
                z_low = keep(lane_z < TRACE, z_right + turned)
                z_high = keep((lane_z >= TRACE) & (lane_z < 2 * TRACE), z_left)
            else:
                pairs = [ordered(k, c) for c in range(cells)]
                z_low, z_high = descend(
                    z_in, z_left, z_right, [p[0] for p in pairs], [p[1] for p in pairs]
                )
            z_in = jnp.where(flag, z_high, z_low)
        entering = [z_in]
        for level in reversed(range(local)):
            following = []
            for index in range(layers >> (level + 1)):
                left = [nodes[node(level, 2 * index, c), :TRACE] for c in range(cells)]
                right = [nodes[node(level, 2 * index + 1, c), :TRACE] for c in range(cells)]
                following += list(
                    descend(
                        entering[index],
                        z_nodes[starts[level] + 2 * index],
                        z_nodes[starts[level] + 2 * index + 1],
                        left,
                        right,
                    )
                )
            entering = following
        for layer in range(layers):
            column = entering[layer].T
            for c in range(cells):
                e = layer * cells + c
                x[e : e + 1, :] = y[e : e + 1, :] + apply(column[: 2 * TRACE, c : c + 1], ends[e])

    for level in range(local):
        for index in range(layers >> level):
            for c in range(cells):
                z_nodes[starts[level] + index, c : c + 1, :] = nodes[node(level, index, c), TRACE : TRACE + 1]
    fall([
        (
            stack([mine[k, c, TRACE : TRACE + 1] for c in range(cells)]),
            stack([theirs[k, c, TRACE : TRACE + 1] for c in range(cells)]),
        )
        for k in range(rounds)
    ])

    x_high, x_low = split(x[...])
    cross = jnp.dot(x_high, pick[...], preferred_element_type=F32) + jnp.dot(
        x_low, pick[...], preferred_element_type=F32
    )
    traces[...] = cross[:, 128:]
    column = cross[:, :128].T
    for e in range(elements):
        backs[e : e + 1, :TRACE] = apply(column[:TRACE, e : e + 1], faces[e, 4])
    up = remote(traces, got_high, cross_sems.at[0], cross_sems.at[1], (place, lax.rem(column_at + 1, width)))
    down = remote(backs, got_back, cross_sems.at[2], cross_sems.at[3], (place, lax.rem(column_at + width - 1, width)))

    @pl.when(column_at < width - 1)
    def _():
        up.start()

    @pl.when(column_at > 0)
    def _():
        down.start()

    for layer in range(layers):
        for c in range(cells):
            e = layer * cells + c
            if c > 0:
                from_left[e : e + 1, :] = traces[e - 1 : e, :]
            if c < cells - 1:
                from_right[e : e + 1, :] = backs[e + 1 : e + 2, :]
    firsts = [layer * cells for layer in range(layers)]
    lasts = [layer * cells + cells - 1 for layer in range(layers)]

    @pl.when(column_at > 0)
    def _():
        up.wait_recv()
        for first, last in zip(firsts, lasts):
            from_left[first : first + 1, :] = got_high[last : last + 1, :]

    @pl.when(column_at == 0)
    def _():
        for first in firsts:
            from_left[first : first + 1, :] = jnp.zeros((1, 128), F32)

    @pl.when(column_at < width - 1)
    def _():
        down.wait_recv()
        for first, last in zip(firsts, lasts):
            from_right[last : last + 1, :] = got_back[first : first + 1, :]

    @pl.when(column_at == width - 1)
    def _():
        for last in lasts:
            from_right[last : last + 1, :] = jnp.zeros((1, 128), F32)

    left_columns = from_left[...].T
    right_columns = from_right[...].T
    lane_row = lanes((1, WIDE))
    for layer in range(layers):
        for c in range(cells):
            e = layer * cells + c
            value = y[e : e + 1, :] - (
                apply(left_columns[:TRACE, e : e + 1], sides[e, :TRACE])
                + apply(right_columns[:TRACE, e : e + 1], sides[e, TRACE:])
            )
            y[e : e + 1, :] = value
            z_nodes[starts[0] + layer, c : c + 1, :] = keep(lane_row < 2 * TRACE, value[:, :WIDE])

    for level in range(local):
        for index in range(layers >> (level + 1)):
            left = [nodes[node(level, 2 * index, c), :TRACE] for c in range(cells)]
            right = [nodes[node(level, 2 * index + 1, c), :TRACE] for c in range(cells)]
            z_nodes[starts[level + 1] + index] = rise(
                z_nodes[starts[level] + 2 * index], z_nodes[starts[level] + 2 * index + 1], left, right
            )
    z_mine[0] = z_nodes[starts[local]]
    for k in range(rounds):
        copy = remote(z_mine.at[k], z_theirs.at[k], z_send.at[k], z_recv.at[k], (partners[k], column_at))
        copy.start()
        sent.append(copy)
        if k < rounds - 1:
            pairs = [ordered(k, c) for c in range(cells)]
        copy.wait_recv()
        if k < rounds - 1:
            flag = bits[k] == 1
            ours, other = z_mine[k], z_theirs[k]
            z_mine[k + 1] = rise(
                jnp.where(flag, other, ours), jnp.where(flag, ours, other),
                [p[0] for p in pairs], [p[1] for p in pairs],
            )
    fall([(z_mine[k], z_theirs[k]) for k in range(rounds)])
    out[...] = x[...]

    for copy in sent:
        copy.wait_send()

    @pl.when(column_at < width - 1)
    def _():
        up.wait_send()

    @pl.when(column_at > 0)
    def _():
        down.wait_send()


def picker():
    table = np.zeros((BLOCK, WIDE), np.float32)
    for slot, i in enumerate(SLOTS):
        for v in range(VARS):
            for k in range(EXTENT):
                source = slot * TRACE + v * FACE + k
                target = v * FACE + i * EXTENT + k
                table[source, target] = 1.0
                table[source + (EXTENT - 1) * EXTENT, 128 + target] = 1.0
    return table


def face_sources():
    nodes_index = np.arange(FACE)
    sources = []
    for variant in range(8):
        first, second = nodes_index // EXTENT, nodes_index % EXTENT
        if variant % 2 == 1:
            first, second = second, first
        if variant // 2 % 2 == 1:
            first = EXTENT - 1 - first
        if variant // 4 % 2 == 1:
            second = EXTENT - 1 - second
        sources.append(first * EXTENT + second)
    source = np.stack(sources)
    return (source[:, :, None] == nodes_index).astype(np.float32)


def on_device(width, count, vector, inverses, lift_maps, jacobians, orient):
    layers, cells = vector.shape[:2]
    elements = layers * cells
    rounds = count.bit_length() - 1
    inv = inverses.reshape(elements, VARS, EXTENT, FACE, BLOCK)
    lift_rows = lift_maps.transpose(0, 2, 1).reshape(4 * TRACE, BLOCK)
    lhs = jnp.concatenate(
        [lift_rows, vector.reshape(elements, BLOCK), jnp.zeros((-elements % 16, BLOCK), F32)], axis=0
    )
    chosen = (orient.reshape(elements, 1) == jnp.arange(8, dtype=jnp.int32)).astype(F32)
    oriented = jnp.sum(chosen[:, :, None, None] * jnp.asarray(face_sources()), axis=1)
    same = jnp.broadcast_to(jnp.eye(FACE, dtype=F32), (elements, FACE, FACE))
    source_maps = jnp.stack([same, same, oriented, same], axis=1)
    turned = jacobians.reshape(elements, 4, VARS, VARS, FACE).transpose(0, 1, 3, 2, 4)
    faces = (
        turned[:, :, :, None, :, :] * source_maps.transpose(0, 1, 3, 2)[:, :, None, :, None, :]
    ).reshape(elements, 4, TRACE, TRACE)
    back = (jnp.eye(VARS, dtype=F32)[:, None, :, None] * oriented[:, None, :, None, :]).reshape(
        elements, 1, TRACE, TRACE
    )
    faces = jnp.concatenate([faces, back], axis=1)
    pick = jnp.asarray(picker(), BF16)
    total_nodes = 2 * layers - 1
    vmem = pl.BlockSpec(memory_space=pltpu.VMEM)
    result = pl.pallas_call(
        functools.partial(kernel, layers, cells, count, width, rounds),
        out_shape=jax.ShapeDtypeStruct((elements, BLOCK), F32),
        in_specs=[pl.BlockSpec(memory_space=pl.ANY), vmem, vmem, vmem],
        out_specs=vmem,
        scratch_shapes=[
            pltpu.VMEM((elements, EXTENT, VARS, FACE, BLOCK), F32),
            pltpu.SemaphoreType.DMA((elements, EXTENT)),
            pltpu.VMEM(lhs.shape, BF16),
            pltpu.VMEM(lhs.shape, BF16),
            pltpu.VMEM((elements, 2 * TRACE, BLOCK), F32),
            pltpu.VMEM((elements, 2 * TRACE, BLOCK), F32),
            pltpu.VMEM((elements, 2 * TRACE, BLOCK), F32),
            pltpu.VMEM((elements, BLOCK), F32),
            pltpu.VMEM((elements, BLOCK), F32),
            pltpu.VMEM((total_nodes * cells, ROWS, WIDE), F32),
            pltpu.VMEM((total_nodes, 8, WIDE), F32),
            pltpu.VMEM((rounds, cells, ROWS, WIDE), F32),
            pltpu.VMEM((rounds, cells, ROWS, WIDE), F32),
            pltpu.SemaphoreType.DMA((rounds,)),
            pltpu.SemaphoreType.DMA((rounds,)),
            pltpu.SemaphoreType.DMA((2,)),
            pltpu.VMEM((rounds, 8, WIDE), F32),
            pltpu.VMEM((rounds, 8, WIDE), F32),
            pltpu.SemaphoreType.DMA((rounds,)),
            pltpu.SemaphoreType.DMA((rounds,)),
            pltpu.VMEM((elements, 128), F32),
            pltpu.VMEM((elements, 128), F32),
            pltpu.VMEM((elements, 128), F32),
            pltpu.VMEM((elements, 128), F32),
            pltpu.VMEM((elements, 128), F32),
            pltpu.VMEM((elements, 128), F32),
            pltpu.SemaphoreType.DMA((4,)),
        ],
        compiler_params=pltpu.CompilerParams(
            collective_id=0, has_side_effects=True, vmem_limit_bytes=48 * 1024 * 1024
        ),
    )(inv, lhs, faces, pick)
    cube = result.reshape(elements, EXTENT, VARS, FACE)
    order = [SLOTS.index(i) for i in range(EXTENT)]
    natural = jnp.stack([cube[:, slot] for slot in order], axis=2)
    return natural.reshape(layers, cells, BLOCK)


def solution(mesh):
    in_specs = (
        P("stream", "cross", None),
        P("stream", "cross", None, None),
        P(),
        P("stream", "cross", None, None, None, None),
        P("stream", "cross"),
    )
    out_specs = P("stream", "cross", None)
    return jax.shard_map(
        functools.partial(on_device, mesh.shape["cross"], mesh.shape["stream"]),
        mesh=mesh, in_specs=in_specs, out_specs=out_specs, check_vma=False,
    )
```

profile of v0, /device:TPU:0, one launch (start us, length us, event | category | flops | bytes accessed | tf_op | source)
XLA Modules:
  0.0 73.4 jit_solution(16755659159328733138)
XLA Ops:
  0.0 0.8 %copy.31 = s32[4,2]{1,0:T(4,128)S(1)} copy(s32[4,2]{0,1:T(2,128)} %param.11) | data formatting | bytes 64 | tf_op args[4]
  0.8 0.1 eq.34
  0.9 0.1 fusion.1
  0.9 1.0 %multiply_reduce_fusion = f32[8,16,16]{2,1,0:T(8,128)S(1)} fusion(f32[8,16,16]{2,1,0:T(8,128)} %constant.2.clone, f32[8,8]{1,0:T(8,128)S(1)} %fusion.1), kind=kLoop, calls=%fused_computation.2 | loop fusion | flops 30720 | bytes 16640 | tf_op jit(solution)/shard_map/reduce_sum | solution.py:444
  2.0 0.1 copy.32
  2.1 1.1 %copy.30 = f32[8,4,5,5,16]{4,3,2,1,0:T(8,128)S(1)} copy(f32[8,4,5,5,16]{4,1,2,3,0:T(4,128)} %bitcast.29) | data formatting | bytes 102400 | tf_op jit(solution)/shard_map/transpose | solution.py:447
  3.2 5.6 %broadcast_multiply_fusion = f32[8,4,5,16,5,16]{5,4,3,2,1,0:T(8,128)} fusion(f32[8,4,16,16]{3,2,1,0:T(8,128)S(1)} %copy.32, f32[8,4,5,5,16]{4,3,2,1,0:T(8,128)S(1)} %copy.30), kind=kLoop, calls=%fused_computation | loop fusion | flops 204800 | bytes 903168 | tf_op jit(solution)/shard_map/mul | solution.py:449
  8.8 6.9 %mul.62 = f32[8,4,80,80]{3,2,1,0:T(8,128)} reshape(f32[8,4,5,16,5,16]{5,4,3,2,1,0:T(8,128)} %broadcast_multiply_fusion) | data formatting | bytes 1638400 | tf_op jit(solution)/shard_map/mul | solution.py:449
  15.7 0.3 mul.66
  16.0 0.4 mul.67
  16.5 0.0 copy-start.2
  16.5 0.0 copy-start.1
  16.5 0.1 mul.63
  16.6 0.0 copy-start
  16.6 0.1 mul.64
  16.8 1.4 %pad_maximum_fusion.faces = f32[8,5,80,80]{3,2,1,0:T(8,128)S(1)} fusion(f32[8,1,80,80]{3,2,1,0:T(8,128)S(1)} %bitcast_multiply_fusion, f32[8,4,80,80]{3,2,1,0:T(8,128)} %mul.62), kind=kLoop, calls=%fused_computation.1 | loop fusion | flops 256000 | bytes 2048000 | tf_op jit(solution)/shard_map/concatenate | solution.py:454
  18.2 0.0 copy-done.2
  18.2 0.1 pad.12.clone
  18.3 0.0 copy-done.1
  18.3 0.1 maximum_maximum_fusion.lhs
  18.5 54.1 %shard_map.73 = f32[8,320]{1,0:T(8,128)S(1)} custom-call(f32[8,5,4,16,320]{4,3,2,1,0:T(8,128)} %bitcast.26, f32[336,320]{1,0:T(8,128)S(1)} %maximum_maximum_fusion.lhs, f32[8,5,80,80]{3,2,1,0:T(8,128)S(1)} %pad_maximum_fusion.faces, bf16[320,256]{1,0:T(8,128)(2,1)S(1)} %copy-done), custom_call_target="tpu_custom_call" | custom-call | tf_op jit(solution)/shard_map/pallas_call | solution.py:458
  72.5 0.1 reshape.78
  72.7 0.1 copy.37
  72.7 0.7 reshape.79
  (10 shorter events, 0.1 us)
Async XLA Ops:
  16.5 1.7 %copy-start.2 = (f32[4,2,320]{2,1,0:T(2,128)S(1)}, f32[4,2,320]{2,1,0:T(2,128)}, u32[]{:S(2)}) copy-start(f32[4,2,320]{2,1,0:T(2,128)} %param.7) | copy-start | bytes 30724
  16.5 1.8 %copy-start.1 = (f32[4,320,80]{1,2,0:T(8,128)S(1)}, f32[4,320,80]{1,2,0:T(8,128)}, u32[]{:S(2)}) copy-start(f32[4,320,80]{1,2,0:T(8,128)} %param.9) | copy-start | bytes 1228804
  16.6 1.8 %copy-start = (bf16[320,256]{1,0:T(8,128)(2,1)S(1)}, bf16[320,256]{1,0:T(8,128)(2,1)}, u32[]{:S(2)}) copy-start(bf16[320,256]{1,0:T(8,128)(2,1)} %constant.8.clone.pick) | copy-start | bytes 491524
where the time goes:
time: 73.8 us; the launch traced here: 73.4 us
  Pallas kernels  54.1 us (73%)
  local copies, waits for them, and re-layouts  10.9 us (15%)
  other arithmetic  8.31 us (11%)
    pallas_call x1, Pallas kernels, on_device(): pl.pallas_call(functools.partial(kernel, layers, cells, count, width, rou...  54.1 us
    mul x1, local copies, waits for them, and re-layouts, on_device(): turned[:, :, :, None, :, :]  6.9 us
    mul x1, other arithmetic, on_device(): turned[:, :, :, None, :, :]  5.63 us

commit v1 on v0

--- a/solution.py
+++ b/solution.py
@@ -115,8 +115,8 @@
 
 def kernel(
     layers, cells, count, width, rounds,
-    inv, lhs, faces, pick, out,
-    blocks, block_sem, lhs_high, lhs_low, lifted, ends, sides, y, x,
+    inv, vector, lift_maps, jacobians, orient, pick, out,
+    blocks, block_sem, lhs, jac_rows, natural, lhs_high, lhs_low, lifted, ends, sides, y, x,
     nodes, z_nodes, mine, theirs, send_sem, recv_sem, tail_sems,
     z_mine, z_theirs, z_send, z_recv,
     traces, backs, got_high, got_back, from_left, from_right, cross_sems,
@@ -146,6 +146,14 @@
     def _():
         pl.semaphore_signal(barrier, inc=1, device_id=(place, column_at + 1), device_id_type=pl.DeviceIdType.MESH)
 
+    for m in range(4):
+        lhs[m * TRACE : (m + 1) * TRACE, :] = lift_maps[m]
+    lhs[4 * TRACE :, :] = jnp.zeros((lhs.shape[0] - 4 * TRACE, BLOCK), F32)
+    for e in range(elements):
+        lhs[4 * TRACE + e : 4 * TRACE + e + 1, :] = vector[e // cells, e % cells : e % cells + 1, :]
+        for v in range(VARS):
+            for w in range(VARS):
+                jac_rows[e, w, :4, v * FACE : (v + 1) * FACE] = jacobians[e, v, w]
     high, low = split(lhs[...])
     lhs_high[...] = high
     lhs_low[...] = low
@@ -155,7 +163,33 @@
 
     lane = lanes((TRACE, WIDE))
 
-    def prepare(e, carry):
+    row_face = rows((TRACE, TRACE))
+    lane_face = lanes((TRACE, TRACE))
+    same = lax.rem(row_face, FACE) == lax.rem(lane_face, FACE)
+
+    def source_of(code, node_index):
+        first, second = node_index // EXTENT, lax.rem(node_index, EXTENT)
+        first, second = (
+            first + lax.rem(code, 2) * (second - first),
+            second + lax.rem(code, 2) * (first - second),
+        )
+        first = first + lax.rem(code // 2, 2) * (EXTENT - 1 - 2 * first)
+        second = second + lax.rem(code // 4, 2) * (EXTENT - 1 - 2 * second)
+        return first * EXTENT + second
+
+    def face(e, m, chosen):
+        tall = jnp.concatenate(
+            [jnp.broadcast_to(jac_rows[e, w, m : m + 1, :TRACE], (FACE, TRACE)) for w in range(VARS)],
+            axis=0,
+        )
+        return keep(chosen, tall)
+
+    def prepare_layer(layer, carry):
+        for c in range(cells):
+            prepare(layer * cells + c)
+        return carry
+
+    def prepare(e):
         for slot, i in enumerate(SLOTS):
             pltpu.make_async_copy(inv.at[e, :, i], blocks.at[e, slot], block_sem.at[e, slot]).wait()
         block = split(blocks[e].reshape(BLOCK, BLOCK))
@@ -164,8 +198,8 @@
         own = jnp.sum(keep(rows(row_values.shape) == e, row_values), axis=0, keepdims=True)
         y[pl.ds(e, 1), :] = own
         lifted[e] = through[2 * TRACE : 4 * TRACE]
-        upward = -product(split(faces[e, 0]), split(through[:TRACE]))
-        downward = -product(split(faces[e, 1]), split(through[TRACE : 2 * TRACE]))
+        upward = -product(split(face(e, 0, same)), split(through[:TRACE]))
+        downward = -product(split(face(e, 1, same)), split(through[TRACE : 2 * TRACE]))
         ends[e, :TRACE] = downward
         ends[e, TRACE:] = upward
         matrix = keep(lane < 2 * TRACE, upward[:, :WIDE]) + pltpu.roll(
@@ -174,9 +208,11 @@
         nodes[e, :TRACE] = matrix
         bottom = keep(lanes((8, WIDE)) < 2 * TRACE, jnp.broadcast_to(own[:, :WIDE], (8, WIDE)))
         nodes[e, TRACE:] = keep(rows((8, WIDE)) == 0, bottom)
-        return carry
-
-    lax.fori_loop(0, elements, prepare, 0)
+
+    lax.fori_loop(0, layers, prepare_layer, 0)
+
+    sides_met = jnp.minimum(column_at, 1) + jnp.minimum(width - 1 - column_at, 1)
+    pl.semaphore_wait(barrier, rounds + sides_met)
 
     starts = []
     base = 0
@@ -187,59 +223,62 @@
     def node(level, index, c):
         return (starts[level] + index) * cells + c
 
-    for level in range(local):
-        for index in range(layers >> (level + 1)):
-            for c in range(cells):
-                nodes[node(level + 1, index, c)] = join(
-                    nodes[node(level, 2 * index, c)], nodes[node(level, 2 * index + 1, c)]
-                )
-    for c in range(cells):
-        mine[0, c] = nodes[node(local, 0, c)]
-
-    sides_met = jnp.minimum(column_at, 1) + jnp.minimum(width - 1 - column_at, 1)
-    pl.semaphore_wait(barrier, rounds + sides_met)
-
     def remote(source, target, send, recv, device):
         return pltpu.make_async_remote_copy(
             src_ref=source, dst_ref=target, send_sem=send, recv_sem=recv,
             device_id=device, device_id_type=pl.DeviceIdType.MESH,
         )
 
-    def prepare_sides(e, carry):
-        for side in range(2):
-            span = slice(side * TRACE, (side + 1) * TRACE)
-            sides[e, span] = product(split(faces[e, 2 + side]), split(lifted[e, span]))
-        return carry
-
     sent = []
-    for k in range(rounds):
+    pending = {}
+
+    def dispatch(k, c):
         device = (partners[k], column_at)
+        send, recv = send_sem.at[k, c], recv_sem.at[k, c]
         if k < rounds - 1:
-            pending = [remote(mine.at[k], theirs.at[k], send_sem.at[k], recv_sem.at[k], device)]
+            pending[k, c] = [remote(mine.at[k, c], theirs.at[k, c], send, recv, device)]
         else:
-            pending = [
+            first, second = pl.ds(0, 128), pl.ds(128, 128)
+            bottom = pl.ds(TRACE, 8)
+            pending[k, c] = [
+                remote(mine.at[k, c, :, first], theirs.at[k, c, :, first], send, recv, device),
                 remote(
-                    mine.at[k, :, :, pl.ds(0, 128)], theirs.at[k, :, :, pl.ds(0, 128)],
-                    send_sem.at[k], recv_sem.at[k], device,
-                ),
-                remote(
-                    mine.at[k, :, pl.ds(TRACE, 8), pl.ds(128, 128)],
-                    theirs.at[k, :, pl.ds(TRACE, 8), pl.ds(128, 128)],
-                    tail_sems.at[0], tail_sems.at[1], device,
+                    mine.at[k, c, bottom, second], theirs.at[k, c, bottom, second],
+                    tail_sems.at[0, c], tail_sems.at[1, c], device,
                 ),
             ]
-        for copy in pending:
+        for copy in pending[k, c]:
             copy.start()
-        sent += pending
-        if k == 0:
-            lax.fori_loop(0, elements, prepare_sides, 0)
-        for copy in pending:
-            copy.wait_recv()
-        if k < rounds - 1:
-            flag = bits[k] == 1
-            for c in range(cells):
+            sent.append(copy)
+
+    for c in range(cells):
+        for level in range(local):
+            for index in range(layers >> (level + 1)):
+                nodes[node(level + 1, index, c)] = join(
+                    nodes[node(level, 2 * index, c)], nodes[node(level, 2 * index + 1, c)]
+                )
+        mine[0, c] = nodes[node(local, 0, c)]
+        dispatch(0, c)
+
+    def prepare_sides(layer, carry):
+        for c in range(cells):
+            e = layer * cells + c
+            chosen = lax.rem(row_face, FACE) == source_of(orient[c, layer], lax.rem(lane_face, FACE))
+            sides[e, :TRACE] = product(split(face(e, 2, chosen)), split(lifted[e, :TRACE]))
+            sides[e, TRACE:] = product(split(face(e, 3, same)), split(lifted[e, TRACE:]))
+        return carry
+
+    lax.fori_loop(0, layers, prepare_sides, 0)
+
+    for k in range(rounds):
+        for c in range(cells):
+            for copy in pending[k, c]:
+                copy.wait_recv()
+            if k < rounds - 1:
+                flag = bits[k] == 1
                 ours, other = mine[k, c], theirs[k, c]
                 mine[k + 1, c] = join(jnp.where(flag, other, ours), jnp.where(flag, ours, other))
+                dispatch(k + 1, c)
 
     def ordered(k, c):
         flag = bits[k] == 1
@@ -309,7 +348,10 @@
     traces[...] = cross[:, 128:]
     column = cross[:, :128].T
     for e in range(elements):
-        backs[e : e + 1, :TRACE] = apply(column[:TRACE, e : e + 1], faces[e, 4])
+        turn = (row_face // FACE == lane_face // FACE) & (
+            source_of(orient[e % cells, e // cells], lax.rem(row_face, FACE)) == lax.rem(lane_face, FACE)
+        )
+        backs[e : e + 1, :TRACE] = apply(column[:TRACE, e : e + 1], turn.astype(F32))
     up = remote(traces, got_high, cross_sems.at[0], cross_sems.at[1], (place, lax.rem(column_at + 1, width)))
     down = remote(backs, got_back, cross_sems.at[2], cross_sems.at[3], (place, lax.rem(column_at + width - 1, width)))
 
@@ -389,7 +431,13 @@
                 [p[0] for p in pairs], [p[1] for p in pairs],
             )
     fall([(z_mine[k], z_theirs[k]) for k in range(rounds)])
-    out[...] = x[...]
+    for slot, i in enumerate(SLOTS):
+        for v in range(VARS):
+            target = (v * EXTENT + i) * FACE
+            source = slot * TRACE + v * FACE
+            natural[:, target : target + FACE] = x[:, source : source + FACE]
+    for layer in range(layers):
+        out[layer] = natural[layer * cells : (layer + 1) * cells, :]
 
     for copy in sent:
         copy.wait_send()
@@ -415,56 +463,32 @@
     return table
 
 
-def face_sources():
-    nodes_index = np.arange(FACE)
-    sources = []
-    for variant in range(8):
-        first, second = nodes_index // EXTENT, nodes_index % EXTENT
-        if variant % 2 == 1:
-            first, second = second, first
-        if variant // 2 % 2 == 1:
-            first = EXTENT - 1 - first
-        if variant // 4 % 2 == 1:
-            second = EXTENT - 1 - second
-        sources.append(first * EXTENT + second)
-    source = np.stack(sources)
-    return (source[:, :, None] == nodes_index).astype(np.float32)
-
-
 def on_device(width, count, vector, inverses, lift_maps, jacobians, orient):
     layers, cells = vector.shape[:2]
     elements = layers * cells
     rounds = count.bit_length() - 1
     inv = inverses.reshape(elements, VARS, EXTENT, FACE, BLOCK)
-    lift_rows = lift_maps.transpose(0, 2, 1).reshape(4 * TRACE, BLOCK)
-    lhs = jnp.concatenate(
-        [lift_rows, vector.reshape(elements, BLOCK), jnp.zeros((-elements % 16, BLOCK), F32)], axis=0
-    )
-    chosen = (orient.reshape(elements, 1) == jnp.arange(8, dtype=jnp.int32)).astype(F32)
-    oriented = jnp.sum(chosen[:, :, None, None] * jnp.asarray(face_sources()), axis=1)
-    same = jnp.broadcast_to(jnp.eye(FACE, dtype=F32), (elements, FACE, FACE))
-    source_maps = jnp.stack([same, same, oriented, same], axis=1)
-    turned = jacobians.reshape(elements, 4, VARS, VARS, FACE).transpose(0, 1, 3, 2, 4)
-    faces = (
-        turned[:, :, :, None, :, :] * source_maps.transpose(0, 1, 3, 2)[:, :, None, :, None, :]
-    ).reshape(elements, 4, TRACE, TRACE)
-    back = (jnp.eye(VARS, dtype=F32)[:, None, :, None] * oriented[:, None, :, None, :]).reshape(
-        elements, 1, TRACE, TRACE
-    )
-    faces = jnp.concatenate([faces, back], axis=1)
+    flat = jacobians.transpose(0, 1, 3, 4, 2, 5).reshape(elements, VARS, VARS, 4, FACE)
     pick = jnp.asarray(picker(), BF16)
     total_nodes = 2 * layers - 1
+    depth = 4 * TRACE + -(-elements // 16) * 16
     vmem = pl.BlockSpec(memory_space=pltpu.VMEM)
     result = pl.pallas_call(
         functools.partial(kernel, layers, cells, count, width, rounds),
-        out_shape=jax.ShapeDtypeStruct((elements, BLOCK), F32),
-        in_specs=[pl.BlockSpec(memory_space=pl.ANY), vmem, vmem, vmem],
+        out_shape=jax.ShapeDtypeStruct((layers, cells, BLOCK), F32),
+        in_specs=[
+            pl.BlockSpec(memory_space=pltpu.HBM), vmem, vmem, vmem,
+            pl.BlockSpec(memory_space=pltpu.SMEM), vmem,
+        ],
         out_specs=vmem,
         scratch_shapes=[
             pltpu.VMEM((elements, EXTENT, VARS, FACE, BLOCK), F32),
             pltpu.SemaphoreType.DMA((elements, EXTENT)),
-            pltpu.VMEM(lhs.shape, BF16),
-            pltpu.VMEM(lhs.shape, BF16),
+            pltpu.VMEM((depth, BLOCK), F32),
+            pltpu.VMEM((elements, VARS, 8, 128), F32),
+            pltpu.VMEM((elements, BLOCK), F32),
+            pltpu.VMEM((depth, BLOCK), BF16),
+            pltpu.VMEM((depth, BLOCK), BF16),
             pltpu.VMEM((elements, 2 * TRACE, BLOCK), F32),
             pltpu.VMEM((elements, 2 * TRACE, BLOCK), F32),
             pltpu.VMEM((elements, 2 * TRACE, BLOCK), F32),
@@ -474,9 +498,9 @@
             pltpu.VMEM((total_nodes, 8, WIDE), F32),
             pltpu.VMEM((rounds, cells, ROWS, WIDE), F32),
             pltpu.VMEM((rounds, cells, ROWS, WIDE), F32),
-            pltpu.SemaphoreType.DMA((rounds,)),
-            pltpu.SemaphoreType.DMA((rounds,)),
-            pltpu.SemaphoreType.DMA((2,)),
+            pltpu.SemaphoreType.DMA((rounds, cells)),
+            pltpu.SemaphoreType.DMA((rounds, cells)),
+            pltpu.SemaphoreType.DMA((2, cells)),
             pltpu.VMEM((rounds, 8, WIDE), F32),
             pltpu.VMEM((rounds, 8, WIDE), F32),
             pltpu.SemaphoreType.DMA((rounds,)),
@@ -490,13 +514,10 @@
             pltpu.SemaphoreType.DMA((4,)),
         ],
         compiler_params=pltpu.CompilerParams(
-            collective_id=0, has_side_effects=True, vmem_limit_bytes=48 * 1024 * 1024
+            collective_id=0, has_side_effects=True, vmem_limit_bytes=62 * 1024 * 1024
         ),
-    )(inv, lhs, faces, pick)
-    cube = result.reshape(elements, EXTENT, VARS, FACE)
-    order = [SLOTS.index(i) for i in range(EXTENT)]
-    natural = jnp.stack([cube[:, slot] for slot in order], axis=2)
-    return natural.reshape(layers, cells, BLOCK)
+    )(inv, vector, lift_maps.transpose(0, 2, 1), flat, orient.T, pick)
+    return result
 
 
 def solution(mesh):

time: 73.8 us -> 53.4 us (0.72)
  local copies, waits for them, and re-layouts: 10.9 us -> 1.31 us
  other arithmetic: 8.31 us -> 0 us
  Pallas kernels: 54.1 us -> 51.4 us
    mul x5 -> x0, local copies, waits for them, and re-layouts: 7.82 us -> none  [the longest x1 6.9 us: on_device(): turned[:, :, :, None, :, :]]
    mul x2 -> x0, other arithmetic: 5.66 us -> none  [the longest x1 5.63 us: on_device(): turned[:, :, :, None, :, :]]
    pallas_call x1, Pallas kernels: 54.1 us -> 51.4 us  [on_device(): pl.pallas_call(functools.partial(kernel, layers, cells, count, width, rou...]
    concatenate x2 -> x0, other arithmetic: 1.55 us -> none  [the longest x1 1.44 us: on_device(): faces = jnp.concatenate([faces, back], axis=1)]
    transpose x2 -> x0, local copies, waits for them, and re-layouts: 1.22 us -> none  [the longest x1 1.09 us: on_device(): jacobians.reshape(elements, 4, VARS, VARS, FACE).transpose(0, 1, 3, 2, 4)]
    reduce_sum x1 -> x0, other arithmetic: 0.98 us -> none  [on_device(): jnp.sum(chosen[:, :, None, None] * jnp.asarray(face_sources()), axis=1)]
    reshape x3 -> x0, local copies, waits for them, and re-layouts: 0.82 us -> none  [the longest x1 0.72 us: on_device(): return natural.reshape(layers, cells, BLOCK)]
where the time goes in v1:
time: 53.4 us; the launch traced here: 52.7 us
  Pallas kernels  51.4 us (96%)
  local copies, waits for them, and re-layouts  1.31 us (2%)
    pallas_call x1, Pallas kernels, on_device(): pl.pallas_call(functools.partial(kernel, layers, cells, count, width, rou...  51.4 us
    unnamed x1, local copies, waits for them, and re-layouts  1.31 us

profile of v1, /device:TPU:0, one launch (start us, length us, event | category | flops | bytes accessed | tf_op | source)
XLA Modules:
  0.0 52.7 jit_solution(1620183890456439934)
XLA Ops:
  0.0 51.4 %shard_map.64 = f32[4,2,320]{2,1,0:T(2,128)} custom-call(f32[8,5,4,16,320]{4,3,2,1,0:T(8,128)} %bitcast.6, f32[4,2,320]{2,1,0:T(2,128)} %vector.1, f32[4,80,320]{2,1,0:T(8,128)} %bitcast.7, f32[8,5,5,4,16]{4,3,2,1,0:T(4,128)} %bitcast.8, s32[2,4]{1,0:T(2,128)} %bitcast.9, bf16[320,256]{1,0:T(8,128)(2,1)} %constant.2.clone.pick), custom_call_target="tpu_custom_call" | custom-call | tf_op jit(solution)/shard_map/pallas_call | solution.py:476
  51.4 1.3 %copy.8 = f32[4,2,320]{2,1,0:T(2,128)} copy(f32[4,2,320]{2,1,0:T(2,128)} %shard_map.64) | data formatting | bytes 20480

commit v2 on v1

--- a/solution.py
+++ b/solution.py
@@ -119,7 +119,7 @@
     blocks, block_sem, lhs, jac_rows, natural, lhs_high, lhs_low, lifted, ends, sides, y, x,
     nodes, z_nodes, mine, theirs, send_sem, recv_sem, tail_sems,
     z_mine, z_theirs, z_send, z_recv,
-    traces, backs, got_high, got_back, from_left, from_right, cross_sems,
+    turns, traces, backs, got_high, got_back, from_left, from_right, cross_sems,
 ):
     elements = layers * cells
     place = lax.axis_index("stream")
@@ -168,7 +168,8 @@
     same = lax.rem(row_face, FACE) == lax.rem(lane_face, FACE)
 
     def source_of(code, node_index):
-        first, second = node_index // EXTENT, lax.rem(node_index, EXTENT)
+        first = lax.div(node_index, EXTENT)
+        second = node_index - first * EXTENT
         first, second = (
             first + lax.rem(code, 2) * (second - first),
             second + lax.rem(code, 2) * (first - second),
@@ -268,9 +269,21 @@
             sides[e, TRACE:] = product(split(face(e, 3, same)), split(lifted[e, TRACE:]))
         return carry
 
-    lax.fori_loop(0, layers, prepare_sides, 0)
+    def prepare_turns(layer, carry):
+        within = row_face - block_row * FACE
+        for c in range(cells):
+            turn = (block_row == block_lane) & (source_of(orient[c, layer], within) == face_lane)
+            turns[layer * cells + c] = turn.astype(F32)
+        return carry
+
+    block_row, block_lane = lax.div(row_face, FACE), lax.div(lane_face, FACE)
+    face_lane = lane_face - block_lane * FACE
 
     for k in range(rounds):
+        if k == 0:
+            lax.fori_loop(0, layers, prepare_sides, 0)
+        if k == 1 % rounds:
+            lax.fori_loop(0, layers, prepare_turns, 0)
         for c in range(cells):
             for copy in pending[k, c]:
                 copy.wait_recv()
@@ -348,10 +361,7 @@
     traces[...] = cross[:, 128:]
     column = cross[:, :128].T
     for e in range(elements):
-        turn = (row_face // FACE == lane_face // FACE) & (
-            source_of(orient[e % cells, e // cells], lax.rem(row_face, FACE)) == lax.rem(lane_face, FACE)
-        )
-        backs[e : e + 1, :TRACE] = apply(column[:TRACE, e : e + 1], turn.astype(F32))
+        backs[e : e + 1, :TRACE] = apply(column[:TRACE, e : e + 1], turns[e])
     up = remote(traces, got_high, cross_sems.at[0], cross_sems.at[1], (place, lax.rem(column_at + 1, width)))
     down = remote(backs, got_back, cross_sems.at[2], cross_sems.at[3], (place, lax.rem(column_at + width - 1, width)))
 
@@ -505,6 +515,7 @@
             pltpu.VMEM((rounds, 8, WIDE), F32),
             pltpu.SemaphoreType.DMA((rounds,)),
             pltpu.SemaphoreType.DMA((rounds,)),
+            pltpu.VMEM((elements, TRACE, TRACE), F32),
             pltpu.VMEM((elements, 128), F32),
             pltpu.VMEM((elements, 128), F32),
             pltpu.VMEM((elements, 128), F32),

time: 53.4 us -> 53.4 us (level)
  no operation moved by 1% of the time
where the time goes in v2:
time: 53.4 us; the launch traced here: 52.7 us
  Pallas kernels  51.4 us (96%)
  local copies, waits for them, and re-layouts  1.31 us (2%)
    pallas_call x1, Pallas kernels, on_device(): pl.pallas_call(functools.partial(kernel, layers, cells, count, width, rou...  51.4 us
    unnamed x1, local copies, waits for them, and re-layouts  1.31 us

profile of v2, /device:TPU:0, one launch (start us, length us, event | category | flops | bytes accessed | tf_op | source)
XLA Modules:
  0.0 52.7 jit_solution(4606105505033693001)
XLA Ops:
  0.0 51.4 %shard_map.64 = f32[4,2,320]{2,1,0:T(2,128)} custom-call(f32[8,5,4,16,320]{4,3,2,1,0:T(8,128)} %bitcast.6, f32[4,2,320]{2,1,0:T(2,128)} %vector.1, f32[4,80,320]{2,1,0:T(8,128)} %bitcast.7, f32[8,5,5,4,16]{4,3,2,1,0:T(4,128)} %bitcast.8, s32[2,4]{1,0:T(2,128)} %bitcast.9, bf16[320,256]{1,0:T(8,128)(2,1)} %constant.2.clone.pick), custom_call_target="tpu_custom_call" | custom-call | tf_op jit(solution)/shard_map/pallas_call | solution.py:486
  51.4 1.3 %copy.8 = f32[4,2,320]{2,1,0:T(2,128)} copy(f32[4,2,320]{2,1,0:T(2,128)} %shard_map.64) | data formatting | bytes 20480
